TPU v7x, 32 devices: a whole 2x2x4 slice. The times are simulated.
32 devices in a mesh: clip: 8 (over y, x, core), tm: 4 (over z).
Axes of the slice: x: 2, y: 2, z: 4, core: 2. Of those that a mesh axis runs over, the one named last changes fastest.
Arguments:
- latent: bfloat16 [8, 32, 8, 32, 16], P('clip', 'tm'), may hold values from -6 to 6
- offsets: int32 [8], P('clip'), may hold values from 0 to 16
- teacher: bfloat16 [8, 32, 8, 16, 384], P('clip', 'tm'), may hold values from -6 to 6
- w_in: bfloat16 [432, 384], replicated, may hold values from -0.3125 to 0.3125
- w_mid: bfloat16 [10368, 384], P('clip'), may hold values from -0.0625 to 0.0625
Outputs:
- grad_mid: float32 [10368, 384], P('clip')
- grad_in: float32 [432, 384], replicated
Inputs may be any that keep to these rules, and one draw needn't show every extreme that they name: `offsets`: each clip's crop start among the latent columns.
All inputs are finite; a program needn't handle non-finite values.
Results may differ from a plain program's by a relative error of at most 0.00095.
Values may be sent and summed in bfloat16 or wider, within the bound.
No kernel may reach another device: no remote copies, remote signals or barrier semaphores. Data moves between devices by JAX's collectives and lax.ppermute only.
A program may use at most 192 MiB of HBM per device.

v0:
```python
import math
import jax
import jax.numpy as jnp
from jax import lax
from jax.sharding import PartitionSpec as P


def passed_along(block, axis, distance):
    devices = range(lax.axis_size(axis))
    route = [(i - distance, i) for i in devices if i - distance in devices]
    return lax.ppermute(block, axis, route)


def tap_masks(count, rows, cols):
    place = jnp.arange(count, dtype=jnp.int32) % (rows * cols)
    row_pos = place // cols
    col_pos = place % cols
    masks = []
    for row_off in range(3):
        for col_off in range(3):
            good_row = (row_pos + row_off - 1 >= 0) & (row_pos + row_off - 1 < rows)
            good_col = (col_pos + col_off - 1 >= 0) & (col_pos + col_off - 1 < cols)
            masks.append((good_row & good_col).astype(jnp.bfloat16).reshape(count, 1))
    return masks


def tap_slices(extended, count, rows, cols, masks):
    margin = jnp.zeros((cols + 1, extended.shape[1]), extended.dtype)
    padded = jnp.concatenate([margin, extended, margin], axis=0)
    plane = rows * cols
    pieces = []
    for depth in range(3):
        for row_off in range(3):
            for col_off in range(3):
                first = depth * plane + row_off * cols + col_off
                pieces.append(padded[first : first + count] * masks[row_off * 3 + col_off])
    return pieces


def cross_dot(left, right):
    return lax.dot_general(
        left, right, (((0,), (0,)), ((), ())), preferred_element_type=jnp.float32
    )


def shards(latent, offsets, teacher, w_in, w_mid):
    frames = teacher.shape[1]
    rows = teacher.shape[2]
    cols = teacher.shape[3]
    chans = teacher.shape[4]
    plane = rows * cols
    count = frames * plane
    lat_chans = latent.shape[4]
    total_cells = lax.axis_size("clip") * lax.axis_size("tm") * count
    scale = 2.0 / math.sqrt(total_cells)
    masks = tap_masks(count, rows, cols)
    crop = lax.dynamic_slice_in_dim(latent[0], offsets[0], cols, axis=2).reshape(count, lat_chans)
    earlier = passed_along(crop[count - 2 * plane :], "tm", 1)
    crop_ext = jnp.concatenate([earlier, crop], axis=0)
    patch_in = jnp.concatenate(tap_slices(crop_ext, count, rows, cols, masks), axis=1)
    z_first = jnp.dot(patch_in, w_in, preferred_element_type=jnp.float32)
    act = jax.nn.silu(z_first).astype(jnp.bfloat16)
    act_prev = passed_along(act[count - 2 * plane :], "tm", 1)
    act_ext = jnp.concatenate([act_prev, act], axis=0)
    act_taps = tap_slices(act_ext, count, rows, cols, masks)
    w_full = lax.all_gather(w_mid, "clip", axis=0, tiled=True)
    output = jnp.zeros((count, chans), jnp.float32)
    for k in range(27):
        output = output + jnp.dot(
            act_taps[k], w_full[k * chans : (k + 1) * chans], preferred_element_type=jnp.float32
        )
    target_rows = teacher[0].reshape(count, chans).astype(jnp.float32)
    grad_low = ((output - target_rows) * scale).astype(jnp.bfloat16)
    local_mid = jnp.concatenate([cross_dot(act_taps[k], grad_low) for k in range(27)], axis=0)
    lead = 2 * plane + cols + 1
    masked_pads = []
    for k in range(9):
        masked_pads.append(jnp.pad(grad_low * masks[k], ((lead, lead), (0, 0))))
    ext_count = count + 2 * plane
    adjoint = jnp.zeros((ext_count, chans), jnp.float32)
    for depth in range(3):
        for row_off in range(3):
            for col_off in range(3):
                k = depth * 9 + row_off * 3 + col_off
                first = (2 - depth) * plane + (2 - row_off) * cols + (2 - col_off)
                piece = masked_pads[row_off * 3 + col_off][first : first + ext_count]
                adjoint = adjoint + lax.dot_general(
                    piece,
                    w_full[k * chans : (k + 1) * chans],
                    (((1,), (1,)), ((), ())),
                    preferred_element_type=jnp.float32,
                )
    outgoing = adjoint[: 2 * plane]
    incoming = passed_along(outgoing.astype(jnp.bfloat16), "tm", -1).astype(outgoing.dtype)
    own = adjoint[2 * plane :]
    dact = jnp.concatenate([own[: count - 2 * plane], own[count - 2 * plane :] + incoming], axis=0)
    sig = jax.nn.sigmoid(z_first)
    dz_first = (dact * sig * (1.0 + z_first * (1.0 - sig))).astype(jnp.bfloat16)
    grad_in = lax.psum(cross_dot(patch_in, dz_first), ("clip", "tm"))
    summed = lax.psum(local_mid, "tm")
    grad_mid = lax.psum_scatter(summed, "clip", scatter_dimension=0, tiled=True)
    return (grad_mid, grad_in)


def solution(mesh):
    return jax.shard_map(
        shards,
        mesh=mesh,
        in_specs=(
            P("clip", "tm", None, None, None),
            P("clip"),
            P("clip", "tm", None, None, None),
            P(),
            P("clip", None),
        ),
        out_specs=(P("clip", None), P()),
        check_vma=False,
    )
```

profile of v0, /device:TPU:0, one launch (start us, length us, event | category | flops | bytes accessed | tf_op | source)
XLA Modules:
  0.0 524.9 jit_solution(12850490637867089896)
XLA Ops:
  9.7 4.9 collective-permute-start
  18.5 2.0 multiply_convert_fusion
  20.5 3.9 collective-permute-start.1
  24.4 3.4 collective-permute-done.1
  27.8 2.3 concatenate.47
  30.2 35.1 %all-gather.2.cloned.1.call-done = bf16[10368,384]{1,0:T(8,128)(2,1)} async-done(((bf16[1296,384]{1,0:T(8,128)(2,1)}), bf16[10368,384]{1,0:T(8,128)(2,1)}) %all-gather.2.cloned.1.call-update) | async-done | bytes 7962640 | tf_op jit(solution)/shard_map/all_gather | solution.py:66
  65.3 3.0 fusion.52
  68.3 2.8 fusion.51
  71.1 2.8 fusion.50
  75.8 1.9 fusion.132
  81.4 1.9 fusion.123
  90.7 1.9 fusion.108
  96.4 2.0 fusion.99
  98.4 1.9 fusion.96
  100.2 2.1 fusion.93
  102.3 1.9 fusion.90
  106.1 1.9 fusion.84
  108.0 1.9 fusion.46
  111.8 1.9 fusion.48
  113.7 1.9 fusion.45
  117.4 17.8 %broadcast_multiply_fusion = (bf16[1024,384]{1,0:T(8,128)(2,1)S(1)}, bf16[1024,384]{1,0:T(8,128)(2,1)S(1)}, bf16[1024,384]{1,0:T(8,128)(2,1)S(1)}, bf16[1024,384...) fusion(bf16[1024]{0:T(1024)(128)(2,1)S(1)} %get-tuple-element.1, ...), kind=kOutput, calls=%fused_computation.165 | convolution fusion | flops 319684608 | bytes 50843648 | tf_op jit(solution)/shard_map/dot_general | solution.py:69
  135.3 3.1 convolution_dynamic-update-slice_fusion.26
  171.2 1.9 convolution_dynamic-update-slice_fusion.5
  181.4 2.0 fusion.4
  183.5 1.9 convolution_add_fusion.25
  185.4 1.9 convolution_add_fusion.24
  187.3 1.9 convolution_add_fusion.23
  210.1 7.5 %collective-permute-done.2 = bf16[256,384]{1,0:T(8,128)(2,1)S(1)} collective-permute-done((bf16[256,384]{1,0:T(8,128)(2,1)S(1)}, bf16[256,384]{1,0:T(8,128)(2,1)S(1)}, u32[]{:S(2)}, u32[]{:S(2)}) %collective-permute-start.2) | collective-permute-done | bytes 196640 | tf_op jit(solution)/shard_map/ppermute | solution.py:11
  219.6 74.8 %reduce-scatter.2.cloned.1.call-done = f32[1296,384]{1,0:T(8,128)} async-done(((f32[10368,384]{1,0:T(8,128)}), f32[1296,384]{1,0:T(8,128)}) %reduce-scatter.2.cloned.1.call-update) | async-done | bytes 1990672 | tf_op jit(solution)/shard_map/reduce_scatter | solution.py:101
  294.4 133.7 %all-reduce.14.cloned.1.call-done = f32[432,384]{1,0:T(8,128)} async-done(((f32[432,384]{1,0:T(8,128)}), f32[432,384]{1,0:T(8,128)}) %all-reduce.14.cloned.1.call-update) | async-done | bytes 663568 | tf_op jit(solution)/shard_map/psum | solution.py:99
  428.1 86.2 %all-reduce.16.cloned.1.call-done = f32[1296,384]{1,0:T(8,128)} async-done(((f32[1296,384]{1,0:T(8,128)}), f32[1296,384]{1,0:T(8,128)}) %all-reduce.16.cloned.1.call-update) | async-done | bytes 1990672 | tf_op jit(solution)/shard_map/psum | solution.py:100
  514.3 3.0 copy.65
  (157 shorter events, 92.3 us)
Async XLA Ops:
  7.2 11.3 %copy-start = (bf16[432,384]{1,0:T(8,128)(2,1)S(1)}, bf16[432,384]{1,0:T(8,128)(2,1)}, u32[]{:S(2)}) copy-start(bf16[432,384]{1,0:T(8,128)(2,1)} %param.8) | copy-start | bytes 995332
  7.2 58.1 %all-gather.2.cloned.1.call-start = ((), (), s32[]{:S(2)}) async-start(), calls=%async_computation.1 | async-start | bytes 8957952 | tf_op jit(solution)/shard_map/all_gather | solution.py:66
  7.9 286.4 %reduce-scatter.2.cloned.1.call-start = ((), (), s32[]{:S(2)}) async-start(), calls=%async_computation.3 | async-start | bytes 17915904 | tf_op jit(solution)/shard_map/reduce_scatter | solution.py:101
  9.7 6.6 %collective-permute-start = (bf16[256,16]{0,1:T(8,128)(2,1)S(1)}, bf16[256,16]{0,1:T(8,128)(2,1)S(1)}, u32[]{:S(2)}, u32[]{:S(2)}) collective-permute-start(bf16[256,16]{0,1:T(8,128)(2,1)S(1)} %slice.384), channel_id=1, source_target_pairs={{0,1},{1,2},{2,3},{4,5},{5,6},{6,7},{8,9},{9,10},{10,11},{12,13},{... | collective-permute-start | bytes 24584 | tf_op jit(solution)/shard_map/ppermute | solution.py:11
  18.5 2.0 copy-start.13
  20.5 7.4 %collective-permute-start.1 = (bf16[256,384]{1,0:T(8,128)(2,1)S(1)}, bf16[256,384]{1,0:T(8,128)(2,1)S(1)}, u32[]{:S(2)}, u32[]{:S(2)}) collective-permute-start(bf16[256,384]{1,0:T(8,128)(2,1)S(1)} %slice.517), channel_id=1, source_target_pairs={{0,1},{1,2},{2,3},{4,5},{5,6},{6,7},{8,9},{9,10},{10,11},{12,13},{... | collective-permute-start | bytes 589832 | tf_op jit(solution)/shard_map/ppermute | solution.py:11
  30.2 43.8 %copy-start.9 = (bf16[1297,384]{1,0:T(8,128)(2,1)}, bf16[1297,384]{1,0:T(8,128)(2,1)S(1)}, u32[]{:S(2)}) copy-start(bf16[1297,384]{1,0:T(8,128)(2,1)S(1)} %concatenate.47) | copy-start | bytes 2988292
  65.3 8.7 %copy-start.2 = (bf16[10368,384]{1,0:T(8,128)(2,1)S(1)}, bf16[10368,384]{1,0:T(8,128)(2,1)}, u32[]{:S(2)}) copy-start(bf16[10368,384]{1,0:T(8,128)(2,1)} %all-gather.2.cloned.1.call-done) | copy-start | bytes 23887876
  135.3 3.1 copy-start.10
  135.3 3.1 copy-start.11
  181.3 2.1 copy-start.7
  181.3 246.8 %all-reduce.14.cloned.1.call-start = ((), (), s32[]{:S(2)}) async-start(), calls=%async_computation.2 | async-start | bytes 1327104 | tf_op jit(solution)/shard_map/psum | solution.py:99
  183.4 1.9 copy-start.6
  183.4 5.7 %slice-start = ((s8[7962624]{0:T(1024)(128)(4,1)}), s8[4194304]{0:T(1024)(128)(4,1)S(1)}, s32[]{:S(2)}) async-start(s8[7962624]{0:T(1024)(128)(4,1)} %bitcast.44), calls=%async_computation.5 | async-start | bytes 8388608
  185.4 1.9 copy-start.5
  185.4 3.8 slice-start.1
  187.3 1.9 copy-start.4
  189.2 1.3 copy-start.3
  192.8 1.3 copy-start.8
  208.5 9.2 %copy-start.14 = (bf16[1024,432]{0,1:T(8,128)(2,1)S(1)}, bf16[1024,432]{0,1:T(8,128)(2,1)}, u32[]{:S(2)}) copy-start(bf16[1024,432]{0,1:T(8,128)(2,1)} %copy-done.13) | copy-start | bytes 2654212
  208.5 9.2 %copy-start.15 = (f32[1024,384]{1,0:T(8,128)S(1)}, f32[1024,384]{1,0:T(8,128)}, u32[]{:S(2)}) copy-start(f32[1024,384]{1,0:T(8,128)} %get-tuple-element.12) | copy-start | bytes 4718596
  208.5 9.2 %collective-permute-start.2 = (bf16[256,384]{1,0:T(8,128)(2,1)S(1)}, bf16[256,384]{1,0:T(8,128)(2,1)S(1)}, u32[]{:S(2)}, u32[]{:S(2)}) collective-permute-start(bf16[256,384]{1,0:T(8,128)(2,1)S(1)} %slice.1014), channel_id=1, source_target_pairs={{1,0},{2,1},{3,2},{5,4},{6,5},{7,6},{9,8},{10,9},{11,10},{13,12},{... | collective-permute-start | bytes 589832 | tf_op jit(solution)/shard_map/ppermute | solution.py:11
  219.5 294.8 %all-reduce.16.cloned.1.call-start = ((), (), s32[]{:S(2)}) async-start(), calls=%async_computation.4 | async-start | bytes 3981312 | tf_op jit(solution)/shard_map/psum | solution.py:100
  428.1 89.2 %copy-start.12 = (f32[432,384]{1,0:T(8,128)S(1)}, f32[432,384]{1,0:T(8,128)}, u32[]{:S(2)}) copy-start(f32[432,384]{1,0:T(8,128)} %all-reduce.14.cloned.1.call-done) | copy-start | bytes 1990660
  514.3 3.9 copy-start.1
Sparse Core Ops, SparseCore 0:
  9.9 55.3 all-gather.1
  181.4 112.8 reduce-scatter.1
  301.0 127.0 all-reduce.13
  430.4 83.9 all-reduce.15
where the time goes:
time: 528 us; the launch traced here: 525 us
  waiting for transfers between devices  342 us (65%)
  matrix products  145 us (27%)
  between operations  15.4 us (3%)
  starting transfers between devices  10.6 us (2%)
  local copies, waits for them, and re-layouts  10 us (2%)
    psum x1, waiting for transfers between devices, shards(): grad_in = lax.psum(cross_dot(patch_in, dz_first), ('clip', 'tm'))  134 us
    psum x1, waiting for transfers between devices, shards(): summed = lax.psum(local_mid, 'tm')  86.2 us
    reduce_scatter x1, waiting for transfers between devices, shards(): grad_mid = lax.psum_scatter(summed, 'clip', scatter_dimension=0, tiled=True)  74.8 us
    dot_general x27, matrix products, shards(): jnp.dot(act_taps[k], w_full[k * chans:(k + 1) * chans], preferred_element...  70 us
    dot_general x28, matrix products, cross_dot(): lax.dot_general(left, right, (((0,), (0,)), ((), ())), preferred_element_...  47.7 us
    all_gather x1, waiting for transfers between devices, shards(): w_full = lax.all_gather(w_mid, 'clip', axis=0, tiled=True)  35.1 us
    dot_general x27, matrix products, shards(): lax.dot_general(piece, w_full[k * chans:(k + 1) * chans], (((1,), (1,)),...  25.7 us
    ppermute x3, waiting for transfers between devices, passed_along(): return lax.ppermute(block, axis, route)  11 us
  transfers between devices with their start and end apart: 7, of which 6 were waited for; matrix products, arithmetic and copies ran while one was open for 7% of the time, Pallas kernels for 0%

commit v1 on v0

--- a/solution.py
+++ b/solution.py
@@ -96,7 +96,7 @@
     dact = jnp.concatenate([own[: count - 2 * plane], own[count - 2 * plane :] + incoming], axis=0)
     sig = jax.nn.sigmoid(z_first)
     dz_first = (dact * sig * (1.0 + z_first * (1.0 - sig))).astype(jnp.bfloat16)
-    grad_in = lax.psum(cross_dot(patch_in, dz_first), ("clip", "tm"))
+    grad_in = lax.psum(lax.psum(cross_dot(patch_in, dz_first), "tm"), "clip")
     summed = lax.psum(local_mid, "tm")
     grad_mid = lax.psum_scatter(summed, "clip", scatter_dimension=0, tiled=True)
     return (grad_mid, grad_in)

time: 528 us -> 473 us (0.90)
  waiting for transfers between devices: 342 us -> 287 us
    psum x1, waiting for transfers between devices: 134 us -> 56.7 us  [shards(): grad_in = lax.psum(lax.psum(cross_dot(patch_in, dz_first), 'tm'), 'clip')]
    psum x1, waiting for transfers between devices: 86.2 us -> 109 us  [shards(): summed = lax.psum(local_mid, 'tm')]
  transfers between devices with their start and end apart: 7 -> 7, of which waited for: 6 -> 6; matrix products, arithmetic and copies ran while one was open for 7% -> 8% of each run, Pallas kernels for 0% -> 0%
where the time goes in v1:
time: 473 us; the launch traced here: 470 us
  waiting for transfers between devices  287 us (61%)
  matrix products  145 us (31%)
  between operations  15.4 us (3%)
  starting transfers between devices  10.6 us (2%)
  local copies, waits for them, and re-layouts  10 us (2%)
    psum x1, waiting for transfers between devices, shards(): summed = lax.psum(local_mid, 'tm')  109 us
    reduce_scatter x1, waiting for transfers between devices, shards(): grad_mid = lax.psum_scatter(summed, 'clip', scatter_dimension=0, tiled=True)  74.9 us
    dot_general x27, matrix products, shards(): jnp.dot(act_taps[k], w_full[k * chans:(k + 1) * chans], preferred_element...  69.9 us
    psum x1, waiting for transfers between devices, shards(): grad_in = lax.psum(lax.psum(cross_dot(patch_in, dz_first), 'tm'), 'clip')  56.7 us
    dot_general x28, matrix products, cross_dot(): lax.dot_general(left, right, (((0,), (0,)), ((), ())), preferred_element_...  47.7 us
    all_gather x1, waiting for transfers between devices, shards(): w_full = lax.all_gather(w_mid, 'clip', axis=0, tiled=True)  35.1 us
    dot_general x27, matrix products, shards(): lax.dot_general(piece, w_full[k * chans:(k + 1) * chans], (((1,), (1,)),...  25.7 us
    ppermute x3, waiting for transfers between devices, passed_along(): return lax.ppermute(block, axis, route)  11 us
  transfers between devices with their start and end apart: 7, of which 6 were waited for; matrix products, arithmetic and copies ran while one was open for 8% of the time, Pallas kernels for 0%

profile of v1, /device:TPU:0, one launch (start us, length us, event | category | flops | bytes accessed | tf_op | source)
XLA Modules:
  0.0 470.3 jit_solution(15622604135744062736)
XLA Ops:
  9.7 4.9 %collective-permute-start = (bf16[256,16]{0,1:T(8,128)(2,1)S(1)}, bf16[256,16]{0,1:T(8,128)(2,1)S(1)}, u32[]{:S(2)}, u32[]{:S(2)}) collective-permute-start(bf16[256,16]{0,1:T(8,128)(2,1)S(1)} %slice.384), channel_id=1, source_target_pairs={{0,1},{1,2},{2,3},{4,5},{5,6},{6,7},{8,9},{9,10},{10,11},{12,13},{... | collective-permute-start | bytes 24584 | tf_op jit(solution)/shard_map/ppermute | solution.py:11
  18.5 2.0 multiply_convert_fusion
  20.5 3.9 collective-permute-start.1
  24.4 3.4 collective-permute-done.1
  27.8 2.3 concatenate.47
  30.2 35.1 %all-gather.2.cloned.1.call-done = bf16[10368,384]{1,0:T(8,128)(2,1)} async-done(((bf16[1296,384]{1,0:T(8,128)(2,1)}), bf16[10368,384]{1,0:T(8,128)(2,1)}) %all-gather.2.cloned.1.call-update) | async-done | bytes 7962640 | tf_op jit(solution)/shard_map/all_gather | solution.py:66
  65.3 3.0 fusion.52
  68.3 2.8 fusion.51
  71.1 2.8 fusion.50
  73.9 1.9 fusion.49
  81.3 1.9 fusion.123
  90.7 1.9 fusion.108
  96.3 1.9 fusion.99
  98.3 1.9 fusion.96
  100.2 2.1 fusion.93
  102.2 1.9 fusion.90
  106.0 1.9 fusion.84
  107.9 1.9 fusion.46
  111.7 1.9 fusion.48
  113.6 1.9 fusion.45
  117.3 17.8 %broadcast_multiply_fusion = (bf16[1024,384]{1,0:T(8,128)(2,1)S(1)}, bf16[1024,384]{1,0:T(8,128)(2,1)S(1)}, bf16[1024,384]{1,0:T(8,128)(2,1)S(1)}, bf16[1024,384...) fusion(bf16[1024]{0:T(1024)(128)(2,1)S(1)} %get-tuple-element.1, ...), kind=kOutput, calls=%fused_computation.165 | convolution fusion | flops 319684608 | bytes 50843648 | tf_op jit(solution)/shard_map/dot_general | solution.py:69
  135.2 3.1 convolution_dynamic-update-slice_fusion.26
  171.1 1.9 convolution_dynamic-update-slice_fusion.5
  181.2 2.0 fusion.4
  183.3 1.9 convolution_add_fusion.25
  185.2 1.9 convolution_add_fusion.24
  187.1 1.9 convolution_add_fusion.23
  210.0 7.5 %collective-permute-done.2 = bf16[256,384]{1,0:T(8,128)(2,1)S(1)} collective-permute-done((bf16[256,384]{1,0:T(8,128)(2,1)S(1)}, bf16[256,384]{1,0:T(8,128)(2,1)S(1)}, u32[]{:S(2)}, u32[]{:S(2)}) %collective-permute-start.2) | collective-permute-done | bytes 196640 | tf_op jit(solution)/shard_map/ppermute | solution.py:11
  219.3 74.9 %reduce-scatter.2.cloned.1.call-done = f32[1296,384]{1,0:T(8,128)} async-done(((f32[10368,384]{1,0:T(8,128)}), f32[1296,384]{1,0:T(8,128)}) %reduce-scatter.2.cloned.1.call-update) | async-done | bytes 1990672 | tf_op jit(solution)/shard_map/reduce_scatter | solution.py:101
  294.3 108.6 %all-reduce.17.cloned.1.call-done = (f32[1296,384]{1,0:T(8,128)}, f32[432,384]{1,0:T(8,128)}) async-done(((f32[1296,384]{1,0:T(8,128)}, f32[432,384]{1,0:T(8,128)}), (f32[1296,384]{1,0:T(8,128)}, f32[432,384]{1,0:T(8,128)})) %all-reduce.17.cloned.1.call-update) | async-done | bytes 2654224 | tf_op jit(solution)/shard_map/psum | solution.py:100
  403.0 56.7 %all-reduce.15.cloned.1.call-done = f32[432,384]{1,0:T(8,128)} async-done(((f32[432,384]{1,0:T(8,128)}), f32[432,384]{1,0:T(8,128)}) %all-reduce.15.cloned.1.call-update) | async-done | bytes 663568 | tf_op jit(solution)/shard_map/psum | solution.py:99
  459.7 3.0 copy.66
  (157 shorter events, 92.2 us)
Async XLA Ops:
  7.2 11.3 %copy-start = (bf16[432,384]{1,0:T(8,128)(2,1)S(1)}, bf16[432,384]{1,0:T(8,128)(2,1)}, u32[]{:S(2)}) copy-start(bf16[432,384]{1,0:T(8,128)(2,1)} %param.8) | copy-start | bytes 995332
  7.2 58.1 %all-gather.2.cloned.1.call-start = ((), (), s32[]{:S(2)}) async-start(), calls=%async_computation.1 | async-start | bytes 8957952 | tf_op jit(solution)/shard_map/all_gather | solution.py:66
  7.9 286.3 %reduce-scatter.2.cloned.1.call-start = ((), (), s32[]{:S(2)}) async-start(), calls=%async_computation.3 | async-start | bytes 17915904 | tf_op jit(solution)/shard_map/reduce_scatter | solution.py:101
  9.7 6.6 %collective-permute-start = (bf16[256,16]{0,1:T(8,128)(2,1)S(1)}, bf16[256,16]{0,1:T(8,128)(2,1)S(1)}, u32[]{:S(2)}, u32[]{:S(2)}) collective-permute-start(bf16[256,16]{0,1:T(8,128)(2,1)S(1)} %slice.384), channel_id=1, source_target_pairs={{0,1},{1,2},{2,3},{4,5},{5,6},{6,7},{8,9},{9,10},{10,11},{12,13},{... | collective-permute-start | bytes 24584 | tf_op jit(solution)/shard_map/ppermute | solution.py:11
  18.5 2.0 copy-start.13
  20.5 7.4 %collective-permute-start.1 = (bf16[256,384]{1,0:T(8,128)(2,1)S(1)}, bf16[256,384]{1,0:T(8,128)(2,1)S(1)}, u32[]{:S(2)}, u32[]{:S(2)}) collective-permute-start(bf16[256,384]{1,0:T(8,128)(2,1)S(1)} %slice.517), channel_id=1, source_target_pairs={{0,1},{1,2},{2,3},{4,5},{5,6},{6,7},{8,9},{9,10},{10,11},{12,13},{... | collective-permute-start | bytes 589832 | tf_op jit(solution)/shard_map/ppermute | solution.py:11
  30.2 43.7 %copy-start.9 = (bf16[1297,384]{1,0:T(8,128)(2,1)}, bf16[1297,384]{1,0:T(8,128)(2,1)S(1)}, u32[]{:S(2)}) copy-start(bf16[1297,384]{1,0:T(8,128)(2,1)S(1)} %concatenate.47) | copy-start | bytes 2988292
  65.3 8.6 %copy-start.2 = (bf16[10368,384]{1,0:T(8,128)(2,1)S(1)}, bf16[10368,384]{1,0:T(8,128)(2,1)}, u32[]{:S(2)}) copy-start(bf16[10368,384]{1,0:T(8,128)(2,1)} %all-gather.2.cloned.1.call-done) | copy-start | bytes 23887876
  135.2 3.1 copy-start.10
  135.2 3.1 copy-start.11
  181.2 2.1 copy-start.7
  181.2 221.7 %all-reduce.17.cloned.1.call-start = ((), (), s32[]{:S(2)}) async-start(), calls=%async_computation.4 | async-start | bytes 5308416 | tf_op jit(solution)/shard_map/psum | solution.py:100
  183.3 1.9 copy-start.6
  183.3 5.7 %slice-start = ((s8[7962624]{0:T(1024)(128)(4,1)}), s8[4194304]{0:T(1024)(128)(4,1)S(1)}, s32[]{:S(2)}) async-start(s8[7962624]{0:T(1024)(128)(4,1)} %bitcast.44), calls=%async_computation.5 | async-start | bytes 8388608
  185.2 1.9 copy-start.5
  185.2 3.8 slice-start.1
  187.1 1.9 copy-start.4
  189.1 1.3 copy-start.3
  192.7 1.3 copy-start.8
  208.3 9.3 %copy-start.14 = (bf16[1024,432]{0,1:T(8,128)(2,1)S(1)}, bf16[1024,432]{0,1:T(8,128)(2,1)}, u32[]{:S(2)}) copy-start(bf16[1024,432]{0,1:T(8,128)(2,1)} %copy-done.13) | copy-start | bytes 2654212
  208.3 9.3 %copy-start.15 = (f32[1024,384]{1,0:T(8,128)S(1)}, f32[1024,384]{1,0:T(8,128)}, u32[]{:S(2)}) copy-start(f32[1024,384]{1,0:T(8,128)} %get-tuple-element.14) | copy-start | bytes 4718596
  208.3 9.2 %collective-permute-start.2 = (bf16[256,384]{1,0:T(8,128)(2,1)S(1)}, bf16[256,384]{1,0:T(8,128)(2,1)S(1)}, u32[]{:S(2)}, u32[]{:S(2)}) collective-permute-start(bf16[256,384]{1,0:T(8,128)(2,1)S(1)} %slice.1014), channel_id=1, source_target_pairs={{1,0},{2,1},{3,2},{5,4},{6,5},{7,6},{9,8},{10,9},{11,10},{13,12},{... | collective-permute-start | bytes 589832 | tf_op jit(solution)/shard_map/ppermute | solution.py:11
  294.2 165.4 %all-reduce.15.cloned.1.call-start = ((), (), s32[]{:S(2)}) async-start(), calls=%async_computation.2 | async-start | bytes 1327104 | tf_op jit(solution)/shard_map/psum | solution.py:99
  459.7 3.1 copy-start.12
  459.7 3.9 copy-start.1
Sparse Core Ops, SparseCore 0:
  9.9 55.3 all-gather.1
  181.3 112.8 reduce-scatter.1
  297.4 105.5 all-reduce.16
  406.3 53.3 all-reduce.14
